TPU v7x, 32 devices: a whole 2x2x4 slice. The times are simulated.
32 devices in a mesh: req: 4 (over z), head: 4 (over y, x), blk: 2 (over core).
Axes of the slice: x: 2, y: 2, z: 4, core: 2. Of those that a mesh axis runs over, the one named last changes fastest.
Arguments:
- group_rows: bfloat16 [8, 256, 2048], P(None, 'req', ('head', 'blk')), may hold values from -6 to 6
- slot_request: int32 [8], replicated, may hold values from 0 to 7, each once
- cache_len: int32 [8], replicated, may hold values from 1 to 512, as said below
- group_len: int32 [8], replicated, may hold values from 1 to 256, as said below
- attn_cache: bfloat16 [2, 8, 512, 2048], P(None, 'req', None, ('head', 'blk')), as said below
- hand_cache: bfloat16 [2, 2, 8, 512, 2048], P('blk', None, None, 'req', 'head'), may hold values from -6 to 6
- query_weight: bfloat16 [2048, 2048], P(None, ('head', 'blk')), may hold values from -0.125 to 0.125
- key_weight: bfloat16 [2048, 2048], P(None, ('head', 'blk')), may hold values from -0.125 to 0.125
- value_weight: bfloat16 [2048, 2048], P(None, ('head', 'blk')), may hold values from -0.125 to 0.125
- out_weight: bfloat16 [2048, 2048], P(('head', 'blk')), may hold values from -0.125 to 0.125
- query_gain: float32 [2048], P(('head', 'blk')), may hold values from 0.5 to 1.5
- key_gain: float32 [2048], P(('head', 'blk')), may hold values from 0.5 to 1.5
- attn_gain: float32 [2048], replicated, may hold values from 0.1 to 1.9
- mlp_gain: float32 [2048], replicated, may hold values from 0.1 to 1.9
- gate_weight: bfloat16 [2048, 4096], P(None, ('head', 'blk')), may hold values from -0.125 to 0.125
- up_weight: bfloat16 [2048, 4096], P(None, ('head', 'blk')), may hold values from -0.125 to 0.125
- down_weight: bfloat16 [4096, 2048], P(('head', 'blk')), may hold values from -0.09375 to 0.09375
Outputs:
- layer_out: bfloat16 [8, 256, 2048], P(None, 'req', ('head', 'blk'))
- relaid: bfloat16 [2, 2, 8, 512, 2048], P('blk', None, 'req', None, 'head')
Inputs may be any that keep to these rules, and one draw needn't show every extreme that they name: `cache_len`: some request has exactly 512 cached tokens. `group_len`: some request has exactly 256 valid new tokens. `attn_cache`: entry s along the request dimension belongs to request slot_request[s]; positions from cache_len of that request on are not read.
All inputs are finite; a program needn't handle non-finite values.
Results may differ from a plain program's by a relative error of at most 0.009.
The roundings to bfloat16 on the way count: a program that leaves them out, or rounds other values in their place, can miss the bound.
Values may be sent and summed in bfloat16 or wider, within the bound.
A program may use at most 128 MiB of HBM per device.

v0:
```python
import jax
import jax.numpy as jnp
from jax import lax
from jax.sharding import PartitionSpec as P

HD = 128
EPSILON = 1e-06
ROPE_BASE = 500000.0


def rotate(values, places):
    half_dim = values.shape[-1] // 2
    frequency = ROPE_BASE ** (-(jnp.arange(half_dim, dtype=jnp.float32) * 2.0 / values.shape[-1]))
    angles = places[..., None].astype(jnp.float32) * frequency
    cosine_part = jnp.cos(angles)[..., None, :]
    sine_part = jnp.sin(angles)[..., None, :]
    first_half = values[..., :half_dim]
    second_half = values[..., half_dim:]
    return jnp.concatenate(
        [
            first_half * cosine_part - second_half * sine_part,
            second_half * cosine_part + first_half * sine_part,
        ],
        axis=-1,
    )


def send_home(blocks, inverse):
    received = lax.all_to_all(blocks, "req", split_axis=1, concat_axis=0, tiled=True)
    return jnp.take(received, inverse, axis=0)


def on_device(
    group_rows,
    slot_request,
    cache_len,
    group_len,
    attn_cache,
    hand_cache,
    query_weight,
    key_weight,
    value_weight,
    out_weight,
    query_gain,
    key_gain,
    attn_gain,
    mlp_gain,
    gate_weight,
    up_weight,
    down_weight,
):
    slot_total = slot_request.shape[0]
    slot_count = slot_total // lax.axis_size("req")
    first_slot = lax.axis_index("req") * slot_count
    own_requests = lax.dynamic_slice_in_dim(slot_request, first_slot, slot_count)
    cached = jnp.take(cache_len, own_requests)
    group_valid = jnp.take(group_len, own_requests)
    inverse = (
        jnp.zeros_like(slot_request).at[slot_request].set(jnp.arange(slot_total, dtype=jnp.int32))
    )
    reordered = jnp.take(hand_cache, slot_request, axis=2)
    relaid = lax.all_to_all(reordered, "req", split_axis=2, concat_axis=3, tiled=True)
    local_x = lax.all_to_all(
        jnp.take(group_rows, slot_request, axis=0), "req", split_axis=0, concat_axis=1, tiled=True
    )
    tokens = local_x.shape[1]
    row_width = local_x.shape[2]
    model_width = row_width * lax.axis_size(("head", "blk"))
    feature_start = lax.axis_index(("head", "blk")) * row_width
    full_x = lax.all_gather(local_x, ("head", "blk"), axis=2, tiled=True)
    rows_x = full_x.reshape(-1, model_width)
    queries = jnp.dot(rows_x, query_weight, preferred_element_type=jnp.float32)
    keys_new = jnp.dot(rows_x, key_weight, preferred_element_type=jnp.float32)
    values_new = jnp.dot(rows_x, value_weight, preferred_element_type=jnp.float32)
    square_sums = lax.psum(
        (jnp.sum(queries * queries, axis=-1), jnp.sum(keys_new * keys_new, axis=-1)),
        ("head", "blk"),
    )
    queries = queries * lax.rsqrt(square_sums[0] / model_width + EPSILON)[:, None] * query_gain
    keys_new = keys_new * lax.rsqrt(square_sums[1] / model_width + EPSILON)[:, None] * key_gain
    heads_here = row_width // HD
    places = cached[:, None] + jnp.arange(tokens, dtype=jnp.int32)[None, :]
    queries = rotate(queries.reshape(slot_count, tokens, heads_here, HD), places).astype(
        jnp.bfloat16
    )
    keys_new = rotate(keys_new.reshape(slot_count, tokens, heads_here, HD), places).astype(
        jnp.bfloat16
    )
    values_new = values_new.astype(jnp.bfloat16).reshape(slot_count, tokens, heads_here, HD)
    keys_old = attn_cache[0].reshape(slot_count, -1, heads_here, HD)
    values_old = attn_cache[1].reshape(slot_count, -1, heads_here, HD)
    score_scale = 1.0 / HD**0.5
    span_old = keys_old.shape[1]
    old_scores = (
        jnp.einsum("sthd,sjhd->shtj", queries, keys_old, preferred_element_type=jnp.float32)
        * score_scale
    )
    new_scores = (
        jnp.einsum("sthd,sjhd->shtj", queries, keys_new, preferred_element_type=jnp.float32)
        * score_scale
    )
    old_mask = (jnp.arange(span_old)[None, :] < cached[:, None])[:, None, None, :]
    columns = jnp.arange(tokens)
    new_mask = (columns[None, None, :] <= columns[None, :, None]) & (
        columns[None, None, :] < group_valid[:, None, None]
    )
    new_mask = new_mask[:, None, :, :]
    scores = jnp.concatenate(
        [jnp.where(old_mask, old_scores, -1e30), jnp.where(new_mask, new_scores, -1e30)], axis=-1
    )
    row_top = jnp.max(scores, axis=-1, keepdims=True)
    weights = jnp.exp(scores - row_top)
    weights = (weights / jnp.sum(weights, axis=-1, keepdims=True)).astype(jnp.bfloat16)
    stacked = jnp.concatenate([values_old, values_new], axis=1)
    attended = jnp.einsum("shtj,sjhd->sthd", weights, stacked, preferred_element_type=jnp.float32)
    attended = attended.astype(jnp.bfloat16).reshape(-1, row_width)
    partial_value = jnp.dot(attended, out_weight, preferred_element_type=jnp.float32)
    totals = lax.psum(partial_value, ("head", "blk"))
    normed = (
        totals * lax.rsqrt(jnp.mean(totals * totals, axis=-1, keepdims=True) + EPSILON) * attn_gain
    )
    state_full = (rows_x.astype(jnp.float32) + normed).astype(jnp.bfloat16)
    state_part = lax.dynamic_slice_in_dim(state_full, feature_start, row_width, 1)
    gate_act = jnp.dot(state_full, gate_weight, preferred_element_type=jnp.float32)
    up_act = jnp.dot(state_full, up_weight, preferred_element_type=jnp.float32)
    inner = (jax.nn.silu(gate_act) * up_act).astype(jnp.bfloat16)
    down_sum = jnp.dot(inner, down_weight, preferred_element_type=jnp.float32)
    down_share = lax.psum_scatter(down_sum, ("head", "blk"), scatter_dimension=1, tiled=True)
    down_power = lax.psum(jnp.sum(down_share * down_share, axis=-1), ("head", "blk"))
    mgain_part = lax.dynamic_slice_in_dim(mlp_gain, feature_start, row_width)
    result = (
        state_part.astype(jnp.float32)
        + down_share * lax.rsqrt(down_power / model_width + EPSILON)[:, None] * mgain_part
    ).astype(jnp.bfloat16)
    layer_out = send_home(result.reshape(slot_count, tokens, row_width), inverse)
    return (layer_out, relaid)


def solution(mesh):
    in_specs = (
        P(None, "req", ("head", "blk")),
        P(),
        P(),
        P(),
        P(None, "req", None, ("head", "blk")),
        P("blk", None, None, "req", "head"),
        P(None, ("head", "blk")),
        P(None, ("head", "blk")),
        P(None, ("head", "blk")),
        P(("head", "blk"), None),
        P(("head", "blk")),
        P(("head", "blk")),
        P(),
        P(),
        P(None, ("head", "blk")),
        P(None, ("head", "blk")),
        P(("head", "blk"), None),
    )
    out_specs = (P(None, "req", ("head", "blk")), P("blk", None, "req", None, "head"))
    return jax.shard_map(
        on_device, mesh=mesh, in_specs=in_specs, out_specs=out_specs, check_vma=False
    )
```

profile of v0, /device:TPU:0, one launch (start us, length us, event | category | flops | bytes accessed | tf_op | source)
XLA Modules:
  0.0 288.7 jit_solution(8035457051612961432)
XLA Ops:
  8.7 1.5 gather_fusion.1
  10.3 15.0 %all_to_all.54 = bf16[8,64,256]{2,1,0:T(8,128)(2,1)S(1)} all-to-all(bf16[8,64,256]{2,1,0:T(8,128)(2,1)S(1)} %broadcast_select_fusion.1), channel_id=1, replica_groups=mesh['req'=4,'head'=4,'blk'=2] {'req'}, dimensions={0} | all-to-all | bytes 524288 | tf_op jit(solution)/shard_map/all_to_all | solution.py:63
  27.5 1.3 fusion.25
  31.2 1.7 multiply_cosine_fusion
  33.0 20.6 %all-gather.2.cloned.1.call-done = bf16[2,256,2048]{2,1,0:T(8,128)(2,1)} async-done(((bf16[2,256,256]{2,1,0:T(8,128)(2,1)}), bf16[2,256,2048]{2,1,0:T(8,128)(2,1)}) %all-gather.2.cloned.1.call-update) | async-done | bytes 2097168 | tf_op jit(solution)/shard_map/all_gather | solution.py:70
  53.6 2.8 multiply_reduce_fusion.2
  56.3 2.8 multiply_reduce_fusion.3
  59.1 13.1 %all-reduce = (f32[512]{0:T(512)S(1)}, f32[512]{0:T(512)S(1)}) all-reduce(f32[512]{0:T(512)S(1)} %get-tuple-element.22, f32[512]{0:T(512)S(1)} %get-tuple-element.24), channel_id=1, replica_groups=mesh['req'=4,'head'=4,'blk'=2] {'head','blk'}, use_global_device_ids=true, to_apply=%region_3.6 | all-reduce | flops 1024 | bytes 8192 | tf_op jit(solution)/shard_map/psum | solution.py:75
  76.7 1.9 multiply_multiply_fusion.1
  78.6 2.2 reshape.152
  80.8 2.0 fusion.26
  82.8 2.0 copy.74
  84.7 1.9 copy.75
  86.7 3.3 %convolution_convert_fusion = bf16[512,256]{1,0:T(8,128)(2,1)} fusion(bf16[512,2048]{1,0:T(8,128)(2,1)} %bitcast.50, bf16[2048,256]{1,0:T(8,128)(2,1)} %param.29), kind=kOutput, calls=%fused_computation.20 | convolution fusion | flops 537001984 | bytes 3407872 | tf_op jit(solution)/shard_map/dot_general | solution.py:74
  90.0 1.7 reshape.151
  91.7 1.8 copy.55
  93.5 1.6 subtract_convert_fusion.1
  97.4 2.0 fusion.6
  100.5 2.7 fusion.12
  103.5 81.0 %all-reduce.3.cloned.1.call-done = f32[512,2048]{1,0:T(8,128)} async-done(((f32[512,2048]{1,0:T(8,128)}), f32[512,2048]{1,0:T(8,128)}) %all-reduce.3.cloned.1.call-update) | async-done | bytes 4194320 | tf_op jit(solution)/shard_map/psum | solution.py:118
  184.4 2.7 multiply_reduce_fusion
  187.9 2.5 add_convert_fusion
  190.4 1.3 copy-done.4
  192.9 7.2 %fusion.7 = f32[512,2048]{1,0:T(8,128)} fusion(bf16[512,2048]{1,0:T(8,128)(2,1)} %param.37, bf16[512,2048]{1,0:T(8,128)(2,1)} %copy-done.4, bf16[2048,512]{1,0:T(8,128)(2,1)} %param.36, f32[512,512]{1,0:T(8,128)S(1)} %fusion.30), kind=kOutput, calls=%fused_computation.22 | convolution fusion | flops 2149056512 | bytes 11534336 | tf_op jit(solution)/shard_map/dot_general | solution.py:127
  200.2 2.0 gather_fusion
  202.2 3.2 %bitcast_select_fusion = bf16[1,2,8,128,512]{4,3,1,0,2:T(8,128)(2,1)} fusion(bf16[8,2,128,512]{3,2,1,0:T(8,128)(2,1)} %gather_fusion, pred[8]{0:T(512)(128)(4,1)S(1)} %compare_and_fusion.2), kind=kLoop, calls=%fused_computation.12 | loop fusion | flops 1048576 | bytes 4194312 | tf_op jit(solution)/shard_map/jit(_take)/select_n | solution.py:61
  205.4 4.6 %all-to-all-start.2 = ((bf16[1,2,8,128,512]{4,3,1,0,2:T(8,128)(2,1)}), bf16[1,2,8,128,512]{4,3,1,0,2:T(8,128)(2,1)}, u32[]{:S(2)}, u32[]{:S(2)}) async-start(bf16[1,2,8,128,512]{4,3,1,0,2:T(8,128)(2,1)} %bitcast_select_fusion), calls=%async_computation.3 | async-start | bytes 4194304 | tf_op jit(solution)/shard_map/all_to_all | solution.py:62
  211.5 40.2 %reduce-scatter.2.cloned.1.call-done = f32[512,256]{1,0:T(8,128)} async-done(((f32[512,2048]{1,0:T(8,128)}), f32[512,256]{1,0:T(8,128)}) %reduce-scatter.2.cloned.1.call-update) | async-done | bytes 524304 | tf_op jit(solution)/shard_map/reduce_scatter | solution.py:128
  253.0 13.1 %psum.31 = f32[512]{0:T(512)S(1)} all-reduce(f32[512]{0:T(512)S(1)} %multiply_reduce_fusion.1), channel_id=1, replica_groups=mesh['req'=4,'head'=4,'blk'=2] {'head','blk'}, use_global_device_ids=true, to_apply=%region_11.14 | all-reduce | flops 512 | bytes 4096 | tf_op jit(solution)/shard_map/psum | solution.py:129
  268.3 4.2 %all-to-all-start.1 = ((bf16[2,256,256]{2,0,1:T(2,128)(2,1)}), bf16[2,256,256]{2,0,1:T(2,128)(2,1)S(1)}, u32[]{:S(2)}, u32[]{:S(2)}) async-start(bf16[2,256,256]{2,0,1:T(2,128)(2,1)} %copy.65), calls=%async_computation.2 | async-start | bytes 524288 | tf_op jit(solution)/shard_map/all_to_all | solution.py:29
  272.5 3.1 %copy.68 = bf16[1,2,2,4,128,512]{5,4,3,2,1,0:T(8,128)(2,1)} copy(bf16[1,2,2,4,128,512]{5,4,1,2,3,0:T(8,128)(2,1)} %bitcast.15) | data formatting | bytes 4194304 | tf_op jit(solution)/shard_map/all_to_all | solution.py:62
  275.6 5.1 %all-to-all-done.1 = bf16[2,256,256]{2,0,1:T(2,128)(2,1)S(1)} async-done(((bf16[2,256,256]{2,0,1:T(2,128)(2,1)}), bf16[2,256,256]{2,0,1:T(2,128)(2,1)S(1)}, u32[]{:S(2)}, u32[]{:S(2)}) %all-to-all-start.1) | async-done | bytes 262176 | tf_op jit(solution)/shard_map/all_to_all | solution.py:29
  (79 shorter events, 22.6 us)
Async XLA Ops:
  7.2 193.0 %copy-start = (bf16[1,2,8,128,512]{4,3,2,1,0:T(8,128)(2,1)S(1)}, bf16[1,2,8,128,512]{4,3,2,1,0:T(8,128)(2,1)}, u32[]{:S(2)}) copy-start(bf16[1,2,8,128,512]{4,3,2,1,0:T(8,128)(2,1)} %param.26) | copy-start | bytes 6291460
  7.2 19.0 %copy-start.12 = (s32[8]{0:T(128)S(1)}, s32[8]{0:T(128)}, u32[]{:S(2)}) copy-start(s32[8]{0:T(128)} %param.22) | copy-start | bytes 100
  7.2 19.0 %copy-start.1 = (s32[8]{0:T(128)S(1)}, s32[8]{0:T(128)}, u32[]{:S(2)}) copy-start(s32[8]{0:T(128)} %param.23) | copy-start | bytes 100
  7.2 19.7 %copy-start.2 = (s32[8]{0:T(128)S(1)}, s32[8]{0:T(128)}, u32[]{:S(2)}) copy-start(s32[8]{0:T(128)} %param.24) | copy-start | bytes 100
  7.2 46.3 %all-gather.2.cloned.1.call-start = ((), (), s32[]{:S(2)}) async-start(), calls=%async_computation.4 | async-start | bytes 2359296 | tf_op jit(solution)/shard_map/all_gather | solution.py:70
  8.1 0.7 copy-start.11
  26.1 158.3 %all-reduce.3.cloned.1.call-start = ((), (), s32[]{:S(2)}) async-start(), calls=%async_computation.5 | async-start | bytes 8388608 | tf_op jit(solution)/shard_map/psum | solution.py:118
  53.6 2.8 copy-start.6
  93.5 1.6 copy-start.5
  96.2 1.0 copy-start.8
  96.2 1.1 copy-start.9
  97.4 3.2 %copy-start.7 = (bf16[256,2048]{1,0:T(8,128)(2,1)S(1)}, bf16[256,2048]{1,0:T(8,128)(2,1)}, u32[]{:S(2)}) copy-start(bf16[256,2048]{1,0:T(8,128)(2,1)} %param.30) | copy-start | bytes 3145732
  103.2 83.9 %copy-start.10 = (f32[2048]{0:T(1024)S(1)}, f32[2048]{0:T(1024)}, u32[]{:S(2)}) copy-start(f32[2048]{0:T(1024)} %param.33) | copy-start | bytes 24580
  103.2 148.5 %reduce-scatter.2.cloned.1.call-start = ((), (), s32[]{:S(2)}) async-start(), calls=%async_computation.6 | async-start | bytes 4718592 | tf_op jit(solution)/shard_map/reduce_scatter | solution.py:128
  184.4 3.4 %copy-start.3 = (f32[512,2048]{1,0:T(8,128)S(1)}, f32[512,2048]{1,0:T(8,128)}, u32[]{:S(2)}) copy-start(f32[512,2048]{1,0:T(8,128)} %all-reduce.3.cloned.1.call-done) | copy-start | bytes 12582916
  187.9 3.8 %copy-start.13 = (bf16[2048,512]{1,0:T(8,128)(2,1)S(1)}, bf16[2048,512]{1,0:T(8,128)(2,1)}, u32[]{:S(2)}) copy-start(bf16[2048,512]{1,0:T(8,128)(2,1)} %param.35) | copy-start | bytes 6291460
  190.3 1.3 copy-start.4
  205.4 62.9 %all-to-all-start.2 = ((bf16[1,2,8,128,512]{4,3,1,0,2:T(8,128)(2,1)}), bf16[1,2,8,128,512]{4,3,1,0,2:T(8,128)(2,1)}, u32[]{:S(2)}, u32[]{:S(2)}) async-start(bf16[1,2,8,128,512]{4,3,1,0,2:T(8,128)(2,1)} %bitcast_select_fusion), calls=%async_computation.3 | async-start | bytes 4194304 | tf_op jit(solution)/shard_map/all_to_all | solution.py:62
  268.3 12.4 %all-to-all-start.1 = ((bf16[2,256,256]{2,0,1:T(2,128)(2,1)}), bf16[2,256,256]{2,0,1:T(2,128)(2,1)S(1)}, u32[]{:S(2)}, u32[]{:S(2)}) async-start(bf16[2,256,256]{2,0,1:T(2,128)(2,1)} %copy.65), calls=%async_computation.2 | async-start | bytes 524288 | tf_op jit(solution)/shard_map/all_to_all | solution.py:29
Sparse Core Ops, SparseCore 0:
  26.2 27.3 all-gather.1
  103.3 81.0 all-reduce.2
  200.3 51.3 reduce-scatter.1
where the time goes:
time: 290 us; the launch traced here: 289 us
  waiting for transfers between devices  147 us (51%)
  blocking collectives  41.2 us (14%)
  local copies, waits for them, and re-layouts  33.5 us (12%)
  matrix products  23.2 us (8%)
  other arithmetic  20.8 us (7%)
  between operations  14 us (5%)
  starting transfers between devices  9.1 us (3%)
    psum x1, waiting for transfers between devices, on_device(): totals = lax.psum(partial_value, ('head', 'blk'))  81 us
    reduce_scatter x1, waiting for transfers between devices, on_device(): lax.psum_scatter(down_sum, ('head', 'blk'), scatter_dimension=1, tiled=True)  40.2 us
    all_gather x1, waiting for transfers between devices, on_device(): full_x = lax.all_gather(local_x, ('head', 'blk'), axis=2, tiled=True)  20.6 us
    all_to_all x1, blocking collectives, on_device(): lax.all_to_all(jnp.take(group_rows, slot_request, axis=0), 'req', split_a...  15 us
    psum x1, blocking collectives, on_device(): lax.psum(jnp.sum(down_share * down_share, axis=-1), ('head', 'blk'))  13.1 us
    psum x1, blocking collectives, on_device(): lax.psum((jnp.sum(queries * queries, axis=-1), jnp.sum(keys_new * keys_ne...  13.1 us
    unnamed x33, local copies, waits for them, and re-layouts  9.4 us
    dot_general x1, matrix products, on_device(): down_sum = jnp.dot(inner, down_weight, preferred_element_type=jnp.float32)  7.24 us
  transfers between devices with their start and end apart: 5, of which 4 were waited for; matrix products, arithmetic and copies ran while one was open for 7% of the time, Pallas kernels for 0%

commit v1 on v0

--- a/solution.py
+++ b/solution.py
@@ -67,7 +67,18 @@
     row_width = local_x.shape[2]
     model_width = row_width * lax.axis_size(("head", "blk"))
     feature_start = lax.axis_index(("head", "blk")) * row_width
-    full_x = lax.all_gather(local_x, ("head", "blk"), axis=2, tiled=True)
+    w1 = lax.axis_size(("head", "blk"))
+    part_now = lax.axis_index(("head", "blk"))
+    mid_arr, aux = (w1, part_now)
+    full_x, main = (local_x, 1)
+    while main < mid_arr:
+        last = lax.ppermute(
+            full_x, axis_name=("head", "blk"), perm=[(i0, i0 ^ main) for i0 in range(mid_arr)]
+        )
+        current_arr = jnp.concatenate([full_x, last], axis=2)
+        v1 = jnp.concatenate([last, full_x], axis=2)
+        full_x = jnp.where(aux & main == 0, current_arr, v1)
+        main = 2 * main
     rows_x = full_x.reshape(-1, model_width)
     queries = jnp.dot(rows_x, query_weight, preferred_element_type=jnp.float32)
     keys_new = jnp.dot(rows_x, key_weight, preferred_element_type=jnp.float32)

time: 290 us -> 313 us (1.079)
  waiting for transfers between devices: 147 us -> 163 us
  blocking collectives: 41.2 us -> 26.4 us
  starting transfers between devices: 9.1 us -> 18.5 us
  other arithmetic: 20.8 us -> 27.8 us
  local copies, waits for them, and re-layouts: 33.5 us -> 39 us
    ppermute x0 -> x3, waiting for transfers between devices: none -> 32.5 us  [on_device(): lax.ppermute(full_x, axis_name=('head', 'blk'), perm=[(i0, i0 ^ main) for...]
    all_gather x1 -> x0, waiting for transfers between devices: 20.6 us -> none  [on_device(): full_x = lax.all_gather(local_x, ('head', 'blk'), axis=2, tiled=True)]
    all_to_all x1 -> x0, blocking collectives: 15 us -> none  [on_device(): lax.all_to_all(jnp.take(group_rows, slot_request, axis=0), 'req', split_a...]
    all_to_all x0 -> x1, waiting for transfers between devices: none -> 6.9 us  [on_device(): lax.all_to_all(jnp.take(group_rows, slot_request, axis=0), 'req', split_a...]
    all_to_all x0 -> x1, starting transfers between devices: none -> 6.32 us  [on_device(): lax.all_to_all(jnp.take(group_rows, slot_request, axis=0), 'req', split_a...]
    ppermute x0 -> x3, starting transfers between devices: none -> 3.21 us  [on_device(): lax.ppermute(full_x, axis_name=('head', 'blk'), perm=[(i0, i0 ^ main) for...]
    unnamed x33 -> x37, local copies, waits for them, and re-layouts: 9.4 us -> 11.7 us
  transfers between devices with their start and end apart: 5 -> 8, of which waited for: 4 -> 6; matrix products, arithmetic and copies ran while one was open for 7% -> 7% of each run, Pallas kernels for 0% -> 0%
where the time goes in v1:
time: 313 us; the launch traced here: 312 us
  waiting for transfers between devices  163 us (52%)
  local copies, waits for them, and re-layouts  39 us (12%)
  other arithmetic  27.8 us (9%)
  blocking collectives  26.4 us (8%)
  matrix products  22.8 us (7%)
  starting transfers between devices  18.5 us (6%)
  between operations  14.3 us (5%)
    psum x1, waiting for transfers between devices, on_device(): totals = lax.psum(partial_value, ('head', 'blk'))  78.3 us
    reduce_scatter x1, waiting for transfers between devices, on_device(): lax.psum_scatter(down_sum, ('head', 'blk'), scatter_dimension=1, tiled=True)  40.2 us
    ppermute x3, waiting for transfers between devices, on_device(): lax.ppermute(full_x, axis_name=('head', 'blk'), perm=[(i0, i0 ^ main) for...  32.5 us
    psum x1, blocking collectives, on_device(): lax.psum((jnp.sum(queries * queries, axis=-1), jnp.sum(keys_new * keys_ne...  13.3 us
    psum x1, blocking collectives, on_device(): lax.psum(jnp.sum(down_share * down_share, axis=-1), ('head', 'blk'))  13.1 us
    unnamed x37, local copies, waits for them, and re-layouts  11.7 us
    dot_general x1, matrix products, on_device(): down_sum = jnp.dot(inner, down_weight, preferred_element_type=jnp.float32)  7.24 us
    all_to_all x1, waiting for transfers between devices, on_device(): lax.all_to_all(jnp.take(group_rows, slot_request, axis=0), 'req', split_a...  6.9 us
  transfers between devices with their start and end apart: 8, of which 6 were waited for; matrix products, arithmetic and copies ran while one was open for 7% of the time, Pallas kernels for 0%

profile of v1, /device:TPU:0, one launch (start us, length us, event | category | flops | bytes accessed | tf_op | source)
XLA Modules:
  0.0 311.8 jit_solution(9282600704694906613)
XLA Ops:
  11.0 6.3 %all-to-all-start = ((bf16[8,64,256]{2,1,0:T(8,128)(2,1)}), bf16[8,64,256]{2,1,0:T(8,128)(2,1)S(1)}, u32[]{:S(2)}, u32[]{:S(2)}) async-start(bf16[8,64,256]{2,1,0:T(8,128)(2,1)} %broadcast_select_fusion.1), calls=%async_computation | async-start | bytes 524288 | tf_op jit(solution)/shard_map/all_to_all | solution.py:63
  19.3 6.9 %all-to-all-done = bf16[8,64,256]{2,1,0:T(8,128)(2,1)S(1)} async-done(((bf16[8,64,256]{2,1,0:T(8,128)(2,1)}), bf16[8,64,256]{2,1,0:T(8,128)(2,1)S(1)}, u32[]{:S(2)}, u32[]{:S(2)}) %all-to-all-start) | async-done | bytes 262176 | tf_op jit(solution)/shard_map/all_to_all | solution.py:63
  34.3 12.6 %collective-permute-done.1 = bf16[2,256,512]{2,1,0:T(8,128)(2,1)S(1)} collective-permute-done((bf16[2,256,512]{2,1,0:T(8,128)(2,1)S(1)}, bf16[2,256,512]{2,1,0:T(8,128)(2,1)S(1)}, u32[]{:S(2)}, u32[]{:S(2)}) %collective-permute-start.1) | collective-permute-done | bytes 524320 | tf_op jit(solution)/shard_map/ppermute | solution.py:75
  52.3 19.8 %collective-permute-done.2 = bf16[2,256,1024]{2,1,0:T(8,128)(2,1)S(1)} collective-permute-done((bf16[2,256,1024]{2,1,0:T(8,128)(2,1)S(1)}, bf16[2,256,1024]{2,1,0:T(8,128)(2,1)S(1)}, u32[]{:S(2)}, u32[]{:S(2)}) %collective-permute-start.2) | collective-permute-done | bytes 1048608 | tf_op jit(solution)/shard_map/ppermute | solution.py:75
  73.8 2.2 multiply_reduce_fusion.3
  76.0 13.3 %all-reduce = (f32[512]{0:T(512)}, f32[512]{0:T(512)}) all-reduce(f32[512]{0:T(512)S(1)} %get-tuple-element.22, f32[512]{0:T(512)} %get-tuple-element.24), channel_id=1, replica_groups=mesh['req'=4,'head'=4,'blk'=2] {'head','blk'}, use_global_device_ids=true, to_apply=%region_3.6 | all-reduce | flops 1024 | bytes 8192 | tf_op jit(solution)/shard_map/psum | solution.py:86
  90.0 2.0 multiply_multiply_fusion
  92.0 2.2 reshape.231
  94.2 2.0 fusion.30
  96.2 2.0 copy.77
  98.1 1.9 copy.78
  100.1 2.0 multiply_multiply_fusion.1
  102.0 2.2 reshape.163
  104.2 2.0 fusion.29
  106.2 2.0 copy.74
  108.2 2.0 copy.75
  110.1 3.3 %convolution_convert_fusion = bf16[512,256]{1,0:T(8,128)(2,1)} fusion(bf16[2048,256]{1,0:T(8,128)(2,1)} %param.29, bf16[512,1024]{1,0:T(8,128)(2,1)} %bitcast.60, bf16[512,1024]{1,0:T(8,128)(2,1)S(1)} %maximum_select_fusion.1, pred[]{:T(512)S(6)} %eq.9), kind=kOutput, calls=%fused_computation.19 | convolution fusion | flops 546439168 | bytes 3407873 | tf_op jit(solution)/shard_map/dot_general | solution.py:85
  116.9 1.9 subtract_convert_fusion.1
  121.1 2.0 fusion.5
  124.3 3.9 %fusion.13 = f32[512,2048]{1,0:T(8,128)} fusion(bf16[256,2048]{1,0:T(8,128)(2,1)} %param.30, bf16[64,8,2,128]{3,2,1,0:T(2,128)(2,1)S(1)} %bitcast.53), kind=kOutput, calls=%fused_computation.44 | convolution fusion | flops 536870912 | bytes 5505024 | tf_op jit(solution)/shard_map/dot_general | solution.py:128
  128.5 78.3 %all-reduce.3.cloned.1.call-done = f32[512,2048]{1,0:T(8,128)} async-done(((f32[512,2048]{1,0:T(8,128)}), f32[512,2048]{1,0:T(8,128)}) %all-reduce.3.cloned.1.call-update) | async-done | bytes 4194320 | tf_op jit(solution)/shard_map/psum | solution.py:129
  206.8 2.7 multiply_reduce_fusion
  210.2 3.0 add_convert_fusion
  215.8 7.2 %fusion.9 = f32[512,2048]{1,0:T(8,128)} fusion(bf16[512,2048]{1,0:T(8,128)(2,1)} %param.37, f32[512,512]{1,0:T(8,128)S(1)} %fusion.33, bf16[512,2048]{1,0:T(8,128)(2,1)} %copy-done.4, bf16[2048,512]{1,0:T(8,128)(2,1)} %param.36), kind=kOutput, calls=%fused_computation.27 | convolution fusion | flops 2149056512 | bytes 11534336 | tf_op jit(solution)/shard_map/dot_general | solution.py:138
  223.1 2.0 gather_fusion
  225.1 3.2 %bitcast_select_fusion = bf16[1,2,8,128,512]{4,3,1,0,2:T(8,128)(2,1)} fusion(bf16[8,2,128,512]{3,2,1,0:T(8,128)(2,1)} %gather_fusion, pred[8]{0:T(512)(128)(4,1)S(1)} %compare_and_fusion.2), kind=kLoop, calls=%fused_computation.13 | loop fusion | flops 1048576 | bytes 4194312 | tf_op jit(solution)/shard_map/jit(_take)/select_n | solution.py:61
  228.3 4.6 %all-to-all-start.2 = ((bf16[1,2,8,128,512]{4,3,1,0,2:T(8,128)(2,1)}), bf16[1,2,8,128,512]{4,3,1,0,2:T(8,128)(2,1)}, u32[]{:S(2)}, u32[]{:S(2)}) async-start(bf16[1,2,8,128,512]{4,3,1,0,2:T(8,128)(2,1)} %bitcast_select_fusion), calls=%async_computation.3 | async-start | bytes 4194304 | tf_op jit(solution)/shard_map/all_to_all | solution.py:62
  234.4 40.2 %reduce-scatter.2.cloned.1.call-done = f32[512,256]{1,0:T(8,128)} async-done(((f32[512,2048]{1,0:T(8,128)}), f32[512,256]{1,0:T(8,128)}) %reduce-scatter.2.cloned.1.call-update) | async-done | bytes 524304 | tf_op jit(solution)/shard_map/reduce_scatter | solution.py:139
  275.8 13.1 %psum.31 = f32[512]{0:T(512)S(1)} all-reduce(f32[512]{0:T(512)S(1)} %multiply_reduce_fusion.1), channel_id=1, replica_groups=mesh['req'=4,'head'=4,'blk'=2] {'head','blk'}, use_global_device_ids=true, to_apply=%region_11.14 | all-reduce | flops 512 | bytes 4096 | tf_op jit(solution)/shard_map/psum | solution.py:140
  291.1 4.2 %all-to-all-start.1 = ((bf16[2,256,256]{2,0,1:T(2,128)(2,1)}), bf16[2,256,256]{2,0,1:T(2,128)(2,1)S(1)}, u32[]{:S(2)}, u32[]{:S(2)}) async-start(bf16[2,256,256]{2,0,1:T(2,128)(2,1)} %copy.65), calls=%async_computation.2 | async-start | bytes 524288 | tf_op jit(solution)/shard_map/all_to_all | solution.py:29
  295.3 3.1 copy.68
  298.4 5.1 %all-to-all-done.1 = bf16[2,256,256]{2,0,1:T(2,128)(2,1)S(1)} async-done(((bf16[2,256,256]{2,0,1:T(2,128)(2,1)}), bf16[2,256,256]{2,0,1:T(2,128)(2,1)S(1)}, u32[]{:S(2)}, u32[]{:S(2)}) %all-to-all-start.1) | async-done | bytes 262176 | tf_op jit(solution)/shard_map/all_to_all | solution.py:29
  (91 shorter events, 38.3 us)
Async XLA Ops:
  7.2 215.9 %copy-start = (bf16[1,2,8,128,512]{4,3,2,1,0:T(8,128)(2,1)S(1)}, bf16[1,2,8,128,512]{4,3,2,1,0:T(8,128)(2,1)}, u32[]{:S(2)}) copy-start(bf16[1,2,8,128,512]{4,3,2,1,0:T(8,128)(2,1)} %param.26) | copy-start | bytes 6291460
  8.0 0.7 copy-start.11
  8.7 19.4 %copy-start.1 = (s32[8]{0:T(128)S(1)}, s32[8]{0:T(128)}, u32[]{:S(2)}) copy-start(s32[8]{0:T(128)} %param.23) | copy-start | bytes 100
  10.2 18.5 %copy-start.2 = (s32[8]{0:T(128)S(1)}, s32[8]{0:T(128)}, u32[]{:S(2)}) copy-start(s32[8]{0:T(128)} %param.24) | copy-start | bytes 100
  11.0 15.2 %all-to-all-start = ((bf16[8,64,256]{2,1,0:T(8,128)(2,1)}), bf16[8,64,256]{2,1,0:T(8,128)(2,1)S(1)}, u32[]{:S(2)}, u32[]{:S(2)}) async-start(bf16[8,64,256]{2,1,0:T(8,128)(2,1)} %broadcast_select_fusion.1), calls=%async_computation | async-start | bytes 524288 | tf_op jit(solution)/shard_map/all_to_all | solution.py:63
  17.3 189.5 %all-reduce.3.cloned.1.call-start = ((), (), s32[]{:S(2)}) async-start(), calls=%async_computation.4 | async-start | bytes 8388608 | tf_op jit(solution)/shard_map/psum | solution.py:129
  19.3 12.0 %copy-start.12 = (s32[8]{0:T(128)S(1)}, s32[8]{0:T(128)}, u32[]{:S(2)}) copy-start(s32[8]{0:T(128)} %param.22) | copy-start | bytes 100
  26.2 0.7 copy-start.6
  27.9 3.5 %collective-permute-start = (bf16[2,256,256]{2,1,0:T(8,128)(2,1)S(1)}, bf16[2,256,256]{2,1,0:T(8,128)(2,1)}, u32[]{:S(2)}, u32[]{:S(2)}) collective-permute-start(bf16[2,256,256]{2,1,0:T(8,128)(2,1)S(1)} %bitcast.47), channel_id=1, source_target_pairs={{0,1},{1,0},{2,3},{3,2},{4,5},{5,4},{6,7},{7,6},{8,9},{9,8},{10,11... | collective-permute-start | bytes 786440 | tf_op jit(solution)/shard_map/ppermute | solution.py:75
  32.6 14.4 %collective-permute-start.1 = (bf16[2,256,512]{2,1,0:T(8,128)(2,1)S(1)}, bf16[2,256,512]{2,1,0:T(8,128)(2,1)S(1)}, u32[]{:S(2)}, u32[]{:S(2)}) collective-permute-start(bf16[2,256,512]{2,1,0:T(8,128)(2,1)S(1)} %maximum_select_fusion.4), channel_id=1, source_target_pairs={{0,2},{1,3},{2,0},{3,1},{4,6},{5,7},{6,4},{7,5},{8,10},{9,11},{10,... | collective-permute-start | bytes 1572872 | tf_op jit(solution)/shard_map/ppermute | solution.py:75
  47.3 24.8 %copy-start.14 = (bf16[2048,256]{1,0:T(8,128)(2,1)S(1)}, bf16[2048,256]{1,0:T(8,128)(2,1)}, u32[]{:S(2)}) copy-start(bf16[2048,256]{1,0:T(8,128)(2,1)} %param.28) | copy-start | bytes 3145732
  47.3 24.8 %collective-permute-start.2 = (bf16[2,256,1024]{2,1,0:T(8,128)(2,1)S(1)}, bf16[2,256,1024]{2,1,0:T(8,128)(2,1)S(1)}, u32[]{:S(2)}, u32[]{:S(2)}) collective-permute-start(bf16[2,256,1024]{2,1,0:T(8,128)(2,1)S(1)} %maximum_select_fusion.2), channel_id=1, source_target_pairs={{0,4},{1,5},{2,6},{3,7},{4,0},{5,1},{6,2},{7,3},{8,12},{9,13},{10,... | collective-permute-start | bytes 3145736 | tf_op jit(solution)/shard_map/ppermute | solution.py:75
  72.1 1.7 copy-start.7
  72.1 1.7 copy-start.15
  116.9 1.9 copy-start.5
  120.0 1.0 copy-start.8
  120.0 1.1 copy-start.9
  128.2 81.3 %copy-start.10 = (f32[2048]{0:T(1024)S(1)}, f32[2048]{0:T(1024)}, u32[]{:S(2)}) copy-start(f32[2048]{0:T(1024)} %param.33) | copy-start | bytes 24580
  128.2 146.4 %reduce-scatter.2.cloned.1.call-start = ((), (), s32[]{:S(2)}) async-start(), calls=%async_computation.5 | async-start | bytes 4718592 | tf_op jit(solution)/shard_map/reduce_scatter | solution.py:139
  206.8 3.4 %copy-start.3 = (f32[512,2048]{1,0:T(8,128)S(1)}, f32[512,2048]{1,0:T(8,128)}, u32[]{:S(2)}) copy-start(f32[512,2048]{1,0:T(8,128)} %all-reduce.3.cloned.1.call-done) | copy-start | bytes 12582916
  210.2 4.3 %copy-start.13 = (bf16[2048,512]{1,0:T(8,128)(2,1)S(1)}, bf16[2048,512]{1,0:T(8,128)(2,1)}, u32[]{:S(2)}) copy-start(bf16[2048,512]{1,0:T(8,128)(2,1)} %param.35) | copy-start | bytes 6291460
  213.2 1.3 copy-start.4
  228.3 62.8 %all-to-all-start.2 = ((bf16[1,2,8,128,512]{4,3,1,0,2:T(8,128)(2,1)}), bf16[1,2,8,128,512]{4,3,1,0,2:T(8,128)(2,1)}, u32[]{:S(2)}, u32[]{:S(2)}) async-start(bf16[1,2,8,128,512]{4,3,1,0,2:T(8,128)(2,1)} %bitcast_select_fusion), calls=%async_computation.3 | async-start | bytes 4194304 | tf_op jit(solution)/shard_map/all_to_all | solution.py:62
  291.1 12.4 %all-to-all-start.1 = ((bf16[2,256,256]{2,0,1:T(2,128)(2,1)}), bf16[2,256,256]{2,0,1:T(2,128)(2,1)S(1)}, u32[]{:S(2)}, u32[]{:S(2)}) async-start(bf16[2,256,256]{2,0,1:T(2,128)(2,1)} %copy.65), calls=%async_computation.2 | async-start | bytes 524288 | tf_op jit(solution)/shard_map/all_to_all | solution.py:29
Sparse Core Ops, SparseCore 0:
  128.4 78.3 all-reduce.2
  223.2 51.3 reduce-scatter.1
